TPU v7x, 512 devices: a whole 4x4x16 slice. The times are simulated.
512 devices in a mesh: ctx: 64 (over z, y), dp: 8 (over x, core).
Axes of the slice: x: 4, y: 4, z: 16, core: 2. Of those that a mesh axis runs over, the one named last changes fastest.
Arguments:
- q_in: bfloat16 [8, 8192, 2048], P('dp', 'ctx'), may hold values from -6 to 6
- k_in: bfloat16 [8, 8192, 2048], P('dp', 'ctx'), may hold values from -6 to 6
- v_in: bfloat16 [8, 8192, 2048], P('dp', 'ctx'), may hold values from -6 to 6
- grad_out: bfloat16 [8, 8192, 2048], P('dp', 'ctx'), may hold values from -6 to 6
- short_filter: float32 [3, 3, 2048], replicated, may hold values from -3.5 to 3.5
- residue: float32 [2048, 8], replicated, may hold values from -2 to 2
- rate: float32 [8], replicated, may hold values from 0.00012207031 to 0.1
Outputs:
- mixed: bfloat16 [8, 8192, 2048], P('dp', 'ctx')
- grad_q: bfloat16 [8, 8192, 2048], P('dp', 'ctx')
- grad_k: bfloat16 [8, 8192, 2048], P('dp', 'ctx')
- grad_v: bfloat16 [8, 8192, 2048], P('dp', 'ctx')
- grad_residue: float32 [2048, 8], P('ctx')
- grad_short: float32 [3, 3, 2048], replicated
All inputs are finite; a program needn't handle non-finite values.
Results may differ from a plain program's by a relative error of at most 0.024.
Values may be sent and summed in bfloat16 or wider, within the bound.
A program may use at most 64 MiB of HBM per device.

v0:
```python
import jax
import jax.numpy as jnp
from jax import lax
from jax.sharding import PartitionSpec as P

BLOCK = 128
PRECISE = lax.Precision.HIGHEST


def passed_along(block, axis, distance):
    devices = range(lax.axis_size(axis))
    route = [(i - distance, i) for i in devices if i - distance in devices]
    return lax.ppermute(block, axis, route)


def mode_sweeps(source, cotangent, rates, columns, gains, front, behind):
    block_len = BLOCK
    block_count = source.shape[1]
    places = jnp.arange(block_len, dtype=jnp.float32)
    offset = places[:, None] - places[None, :]
    blocks = jnp.arange(block_count, dtype=jnp.float32)
    spacing = blocks[:, None] - blocks[None, :] - 1.0
    cot_f = cotangent.astype(jnp.float32)

    def one_mode(carry, item):
        conv_acc, back_acc = carry
        speed, column, start_fwd, start_back = item
        kernel = jnp.where(offset >= 0, jnp.exp(-speed * jnp.maximum(offset, 0.0)), 0.0).astype(
            jnp.bfloat16
        )
        passing = jnp.where(
            spacing >= 0, jnp.exp(-speed * block_len * jnp.maximum(spacing, 0.0)), 0.0
        )
        lead = jnp.exp(-speed * block_len * blocks)
        trail = jnp.exp(-speed * block_len * (block_count - 1.0 - blocks))
        scale_fwd = jnp.exp(-speed * (places + 1.0))
        scale_back = jnp.exp(-speed * (block_len - places))
        inside = jnp.einsum("ts,cns->cnt", kernel, source, preferred_element_type=jnp.float32)
        entering = (
            jnp.einsum("nk,ck->cn", passing, inside[..., block_len - 1], precision=PRECISE)
            + lead[None, :] * start_fwd[:, None]
        )
        forward = inside + scale_fwd[None, None, :] * entering[..., None]
        conv_acc = conv_acc + column[:, None, None] * forward
        grad_row = jnp.sum(forward * cot_f, axis=(1, 2))
        inside_back = jnp.einsum(
            "ts,cnt->cns", kernel, cotangent, preferred_element_type=jnp.float32
        )
        entering_back = (
            jnp.einsum("kn,ck->cn", passing, inside_back[..., 0], precision=PRECISE)
            + trail[None, :] * start_back[:, None]
        )
        backward = inside_back + scale_back[None, None, :] * entering_back[..., None]
        back_acc = back_acc + column[:, None, None] * backward
        return ((conv_acc, back_acc), grad_row)

    zeros_acc = jnp.zeros(source.shape, jnp.float32)
    (conv_sum, back_sum), grads = lax.scan(
        one_mode, (zeros_acc, zeros_acc), (rates, columns, front, behind)
    )
    grads = gains[:, None] * grads
    return (conv_sum, back_sum, grads.T)


def shards(q_in, k_in, v_in, grad_out, short_filter, residue, rate):
    row_count = q_in.shape[1]
    width = q_in.shape[2]
    inputs = (q_in[0], k_in[0], v_in[0])
    tails = jnp.stack([item[row_count - 2 :] for item in inputs])
    before = passed_along(tails, "ctx", 1)
    extended = [
        jnp.concatenate([before[branch], inputs[branch]], axis=0).astype(jnp.float32)
        for branch in range(3)
    ]
    shorts = []
    for branch in range(3):
        total = short_filter[branch, 0][None, :] * extended[branch][2 : 2 + row_count]
        for tap_at in range(1, 3):
            total = (
                total
                + short_filter[branch, tap_at][None, :]
                * extended[branch][2 - tap_at : 2 - tap_at + row_count]
            )
        shorts.append(total)
    query, keyed, valued = shorts
    gated = (keyed * valued).astype(jnp.bfloat16)
    cot_out = grad_out[0].astype(jnp.float32)
    d_conv = (cot_out * query).astype(jnp.bfloat16)
    gains = jnp.sqrt(1.0 - jnp.exp(-2.0 * rate))
    weights = residue * gains[None, :]
    modes = rate.shape[0]
    ctx_count = lax.axis_size("ctx")
    channel_share = width // ctx_count
    owned, incoming = (
        lax.all_to_all(gated, "ctx", split_axis=1, concat_axis=0, tiled=True),
        lax.all_to_all(d_conv, "ctx", split_axis=1, concat_axis=0, tiled=True),
    )
    total_rows = owned.shape[0]
    block_count = total_rows // BLOCK
    owned_lanes = owned.T.reshape(channel_share, block_count, BLOCK)
    incoming_lanes = incoming.T.reshape(channel_share, block_count, BLOCK)
    columns = lax.dynamic_slice_in_dim(
        weights, lax.axis_index("ctx") * channel_share, channel_share, 0
    ).T
    zero_start = jnp.zeros((modes, channel_share), jnp.float32)
    conv_sum, back_sum, partial_value = mode_sweeps(
        owned_lanes, incoming_lanes, rate, columns, gains, zero_start, zero_start
    )
    conv_rows = conv_sum.reshape(channel_share, total_rows).T.astype(jnp.bfloat16)
    back_rows = back_sum.reshape(channel_share, total_rows).T.astype(jnp.bfloat16)
    conv, d_gated = (
        lax.all_to_all(conv_rows, "ctx", split_axis=0, concat_axis=1, tiled=True),
        lax.all_to_all(back_rows, "ctx", split_axis=0, concat_axis=1, tiled=True),
    )
    grad_residue = lax.psum(partial_value, "dp")
    conv_f = conv.astype(jnp.float32)
    mixed = (query * conv_f).astype(jnp.bfloat16)
    gated_back = d_gated.astype(jnp.float32)
    d_shorts = (cot_out * conv_f, gated_back * valued, gated_back * keyed)
    heads = jnp.stack([item[:2] for item in d_shorts])
    after = passed_along(heads.astype(jnp.bfloat16), "ctx", -1).astype(heads.dtype)
    grads = []
    partial_short = []
    for branch in range(3):
        ahead_rows = jnp.concatenate([d_shorts[branch], after[branch]], axis=0)
        total = short_filter[branch, 0][None, :] * ahead_rows[0:row_count]
        for tap_at in range(1, 3):
            total = (
                total
                + short_filter[branch, tap_at][None, :] * ahead_rows[tap_at : tap_at + row_count]
            )
        grads.append(total.astype(jnp.bfloat16)[None])
        partial_short.append(
            jnp.stack(
                [
                    jnp.sum(
                        d_shorts[branch] * extended[branch][2 - tap_at : 2 - tap_at + row_count],
                        axis=0,
                    )
                    for tap_at in range(3)
                ]
            )
        )
    grad_short = lax.psum(jnp.stack(partial_short), ("ctx", "dp"))
    return (mixed[None], grads[0], grads[1], grads[2], grad_residue, grad_short)


def solution(mesh):
    placed = (
        P("dp", "ctx", None),
        P("dp", "ctx", None),
        P("dp", "ctx", None),
        P("dp", "ctx", None),
        P(),
        P(),
        P(),
    )
    return jax.shard_map(
        shards,
        mesh=mesh,
        in_specs=placed,
        out_specs=(
            P("dp", "ctx", None),
            P("dp", "ctx", None),
            P("dp", "ctx", None),
            P("dp", "ctx", None),
            P("ctx", None),
            P(),
        ),
        check_vma=False,
    )
```

profile of v0, /device:TPU:1, one launch (start us, length us, event | category | flops | bytes accessed | tf_op | source)
XLA Modules:
  0.0 703.1 jit_solution(16576350189797462453)
XLA Ops:
  7.2 0.8 slice.139
  7.9 0.8 slice.140
  8.7 0.8 slice.141
  9.5 4.0 collective-permute-start
  13.6 1.0 fusion.78
  14.6 1.3 copy.33
  15.9 1.3 copy.31
  17.9 0.8 maximum_convert_fusion.1
  18.7 4.5 multiply_convert_fusion
  23.2 18.3 %all-to-all-start = ((bf16[128,64,32]{0,2,1:T(8,128)(2,1)}), bf16[128,64,32]{0,2,1:T(8,128)(2,1)S(1)}, u32[]{:S(2)}, u32[]{:S(2)}) async-start(bf16[128,64,32]{0,2,1:T(8,128)(2,1)} %bitcast.16), calls=%async_computation | async-start | bytes 1048576 | tf_op jit(solution)/shard_map/all_to_all | solution.py:95
  42.9 1.3 copy-done.4
  44.2 2.4 fusion.51
  46.6 24.2 %all-to-all-done = bf16[128,64,32]{0,2,1:T(8,128)(2,1)S(1)} async-done(((bf16[128,64,32]{0,2,1:T(8,128)(2,1)}), bf16[128,64,32]{0,2,1:T(8,128)(2,1)S(1)}, u32[]{:S(2)}, u32[]{:S(2)}) %all-to-all-start) | async-done | bytes 524320 | tf_op jit(solution)/shard_map/all_to_all | solution.py:95
  70.7 8.6 %all-to-all-start.1 = ((bf16[128,64,32]{0,2,1:T(8,128)(2,1)}), bf16[128,64,32]{0,2,1:T(8,128)(2,1)S(1)}, u32[]{:S(2)}, u32[]{:S(2)}) async-start(bf16[128,64,32]{0,2,1:T(8,128)(2,1)} %bitcast.20), calls=%async_computation.1 | async-start | bytes 1048576 | tf_op jit(solution)/shard_map/all_to_all | solution.py:96
  79.4 0.8 fusion.77
  80.3 0.9 copy.54
  81.2 27.1 %all-to-all-done.1 = bf16[128,64,32]{0,2,1:T(8,128)(2,1)S(1)} async-done(((bf16[128,64,32]{0,2,1:T(8,128)(2,1)}), bf16[128,64,32]{0,2,1:T(8,128)(2,1)S(1)}, u32[]{:S(2)}, u32[]{:S(2)}) %all-to-all-start.1) | async-done | bytes 524320 | tf_op jit(solution)/shard_map/all_to_all | solution.py:96
  108.4 0.9 copy.55
  109.3 1.1 bitcast_convert_fusion
  110.5 60.8 %while.16 = (s32[]{:T(128)}, f32[32,64,128]{2,1,0:T(8,128)}, f32[32,64,128]{2,1,0:T(8,128)}, f32[8,32]{1,0:T(8,128)S(1)}, f32[8,32]{1,0:T(8,128)S(1)}, /*index=5...) while((s32[]{:T(128)}, f32[32,64,128]{2,1,0:T(8,128)}, ...), condition=%wide.region_2.3_spmd.clone.clone, body=%wide.region_0.2_spmd.clone.clone.sunk | while | flops 140759840 | bytes 12668891 | solution.py:58
  111.8 1.4 convolution_bitcast_fusion.5
  114.9 2.2 multiply_reduce_fusion.11
  118.4 1.4 convolution_bitcast_fusion.5
  121.5 3.3 multiply_reduce_fusion.11
  126.1 1.4 convolution_bitcast_fusion.5
  129.2 3.3 multiply_reduce_fusion.11
  133.8 1.4 convolution_bitcast_fusion.5
  137.0 3.3 multiply_reduce_fusion.11
  141.6 1.4 convolution_bitcast_fusion.5
  144.7 3.3 multiply_reduce_fusion.11
  149.3 1.4 convolution_bitcast_fusion.5
  152.5 3.3 multiply_reduce_fusion.11
  157.1 1.4 convolution_bitcast_fusion.5
  160.2 3.3 multiply_reduce_fusion.11
  164.8 1.4 convolution_bitcast_fusion.5
  167.9 3.3 multiply_reduce_fusion.11
  171.3 1.4 convert_element_type.94
  172.7 1.1 copy_bitcast_fusion
  173.8 9.2 %all-to-all-start.3 = ((bf16[64,128,32]{1,2,0:T(8,128)(2,1)}), bf16[64,128,32]{1,2,0:T(8,128)(2,1)}, u32[]{:S(2)}, u32[]{:S(2)}) async-start(bf16[64,128,32]{1,2,0:T(8,128)(2,1)} %copy_bitcast_fusion), calls=%async_computation.3 | async-start | bytes 1048576 | tf_op jit(solution)/shard_map/all_to_all | solution.py:113
  183.1 1.1 copy_bitcast_fusion.1
  184.3 27.9 %all-to-all-done.3 = bf16[64,128,32]{1,2,0:T(8,128)(2,1)} async-done(((bf16[64,128,32]{1,2,0:T(8,128)(2,1)}), bf16[64,128,32]{1,2,0:T(8,128)(2,1)}, u32[]{:S(2)}, u32[]{:S(2)}) %all-to-all-start.3) | async-done | bytes 524320 | tf_op jit(solution)/shard_map/all_to_all | solution.py:113
  212.1 8.9 %all-to-all-start.2 = ((bf16[64,128,32]{1,2,0:T(8,128)(2,1)}), bf16[64,128,32]{1,2,0:T(8,128)(2,1)}, u32[]{:S(2)}, u32[]{:S(2)}) async-start(bf16[64,128,32]{1,2,0:T(8,128)(2,1)} %copy_bitcast_fusion.1), calls=%async_computation.2 | async-start | bytes 1048576 | tf_op jit(solution)/shard_map/all_to_all | solution.py:112
  221.2 14.6 %psum.14 = f32[32,8]{0,1:T(8,128)} all-reduce(f32[32,8]{0,1:T(8,128)S(1)} %multiply_bitcast_fusion), channel_id=1, replica_groups=mesh['ctx'=64,'dp'=8] {'dp'}, use_global_device_ids=true, to_apply=%region_3.4 | all-reduce | flops 256 | bytes 2048 | tf_op jit(solution)/shard_map/psum | solution.py:115
  235.8 6.3 multiply_reduce_fusion.6
  242.1 1.0 copy-done.7
  243.1 0.8 fusion.72
  243.9 1.2 copy.40
  245.2 0.9 fusion.73
  246.0 1.2 copy.41
  247.3 2.9 all-to-all-done.2
  250.2 3.0 multiply_reduce_fusion.9
  253.5 1.3 collective-permute-start.1
  255.6 1.0 copy.43
  256.6 1.5 collective-permute-done.1
  258.1 0.9 copy.42
  259.4 1.0 copy-done.10
  260.4 2.2 fusion.76
  262.6 2.2 fusion.75
  264.8 2.2 fusion.74
  266.9 1.0 copy.46
  268.0 1.0 copy.45
  269.0 1.0 copy.44
  270.0 424.7 %all-reduce.2.cloned.1.call-done = f32[3,3,2048]{2,1,0:T(4,128)} async-done(((f32[3,3,2048]{2,1,0:T(4,128)}), f32[3,3,2048]{2,1,0:T(4,128)}) %all-reduce.2.cloned.1.call-update) | async-done | bytes 73744 | tf_op jit(solution)/shard_map/psum | solution.py:144
  694.7 1.5 copy.80
  (151 shorter events, 22.3 us)
Async XLA Ops:
  9.5 7.7 %collective-permute-start = (bf16[3,2,2048]{2,1,0:T(2,128)(2,1)S(1)}, bf16[3,2,2048]{2,1,0:T(2,128)(2,1)S(1)}, u32[]{:S(2)}, u32[]{:S(2)}) collective-permute-start(bf16[3,2,2048]{2,1,0:T(2,128)(2,1)S(1)} %pad_maximum_fusion.4), channel_id=1, source_target_pairs={{0,8},{8,16},{16,24},{24,32},{32,40},{40,48},{48,56},{56,64},{64,7... | collective-permute-start | bytes 73736 | tf_op jit(solution)/shard_map/ppermute | solution.py:13
  18.7 4.5 copy-start.1
  18.7 4.5 copy-start.3
  18.7 22.8 %copy-start.13 = (bf16[1,128,2048]{2,1,0:T(8,128)(2,1)S(1)}, bf16[1,128,2048]{2,1,0:T(8,128)(2,1)}, u32[]{:S(2)}) copy-start(bf16[1,128,2048]{2,1,0:T(8,128)(2,1)} %param.9) | copy-start | bytes 1572868
  23.2 18.6 %copy-start.14 = (bf16[1,128,2048]{2,1,0:T(8,128)(2,1)S(1)}, bf16[1,128,2048]{2,1,0:T(8,128)(2,1)}, u32[]{:S(2)}) copy-start(bf16[1,128,2048]{2,1,0:T(8,128)(2,1)} %param.12) | copy-start | bytes 1572868
  23.2 47.5 %all-to-all-start = ((bf16[128,64,32]{0,2,1:T(8,128)(2,1)}), bf16[128,64,32]{0,2,1:T(8,128)(2,1)S(1)}, u32[]{:S(2)}, u32[]{:S(2)}) async-start(bf16[128,64,32]{0,2,1:T(8,128)(2,1)} %bitcast.16), calls=%async_computation | async-start | bytes 1048576 | tf_op jit(solution)/shard_map/all_to_all | solution.py:95
  42.1 4.5 copy-start.11
  42.8 1.4 copy-start.4
  44.2 35.2 %copy-start.15 = (f32[8]{0:T(128)S(1)}, f32[8]{0:T(128)}, u32[]{:S(2)}) copy-start(f32[8]{0:T(128)} %param.15) | copy-start | bytes 100
  70.7 37.6 %all-to-all-start.1 = ((bf16[128,64,32]{0,2,1:T(8,128)(2,1)}), bf16[128,64,32]{0,2,1:T(8,128)(2,1)S(1)}, u32[]{:S(2)}, u32[]{:S(2)}) async-start(bf16[128,64,32]{0,2,1:T(8,128)(2,1)} %bitcast.20), calls=%async_computation.1 | async-start | bytes 1048576 | tf_op jit(solution)/shard_map/all_to_all | solution.py:96
  111.7 2.0 copy-start.6
  118.3 2.0 copy-start.6
  126.1 2.0 copy-start.6
  133.8 2.0 copy-start.6
  141.6 2.0 copy-start.6
  149.3 2.0 copy-start.6
  157.0 2.0 copy-start.6
  164.8 2.0 copy-start.6
  171.3 11.8 %copy-start = (f32[32,64,128]{2,1,0:T(8,128)S(1)}, f32[32,64,128]{2,1,0:T(8,128)}, u32[]{:S(2)}) copy-start(f32[32,64,128]{2,1,0:T(8,128)} %get-tuple-element.87) | copy-start | bytes 3145732
  173.8 38.3 %all-to-all-start.3 = ((bf16[64,128,32]{1,2,0:T(8,128)(2,1)}), bf16[64,128,32]{1,2,0:T(8,128)(2,1)}, u32[]{:S(2)}, u32[]{:S(2)}) async-start(bf16[64,128,32]{1,2,0:T(8,128)(2,1)} %copy_bitcast_fusion), calls=%async_computation.3 | async-start | bytes 1048576 | tf_op jit(solution)/shard_map/all_to_all | solution.py:113
  183.0 52.7 %copy-start.2 = (f32[130,2048]{0,1:T(8,128)S(1)}, f32[130,2048]{0,1:T(8,128)}, u32[]{:S(2)}) copy-start(f32[130,2048]{0,1:T(8,128)} %copy-done.1) | copy-start | bytes 3194884
  212.1 38.0 %all-to-all-start.2 = ((bf16[64,128,32]{1,2,0:T(8,128)(2,1)}), bf16[64,128,32]{1,2,0:T(8,128)(2,1)}, u32[]{:S(2)}, u32[]{:S(2)}) async-start(bf16[64,128,32]{1,2,0:T(8,128)(2,1)} %copy_bitcast_fusion.1), calls=%async_computation.2 | async-start | bytes 1048576 | tf_op jit(solution)/shard_map/all_to_all | solution.py:112
  221.0 473.7 %all-reduce.2.cloned.1.call-start = ((), (), s32[]{:S(2)}) async-start(), calls=%async_computation.4 | async-start | bytes 196608 | tf_op jit(solution)/shard_map/psum | solution.py:144
  242.1 1.0 copy-start.7
  242.1 8.1 %copy-start.9 = (f32[128,2048]{0,1:T(8,128)}, f32[128,2048]{0,1:T(8,128)S(1)}, u32[]{:S(2)}) copy-start(f32[128,2048]{0,1:T(8,128)S(1)} %get-tuple-element.228) | copy-start | bytes 3145732
  242.1 8.0 %copy-start.5 = (f32[130,2048]{0,1:T(8,128)S(1)}, f32[130,2048]{0,1:T(8,128)}, u32[]{:S(2)}) copy-start(f32[130,2048]{0,1:T(8,128)} %copy-done.4) | copy-start | bytes 3194884
  253.2 2.4 copy-start.12
  253.5 4.6 collective-permute-start.1
  259.1 1.2 copy-start.10
  259.4 3.2 copy-start.8
Sparse Core Ops, SparseCore 0:
  255.7 438.9 all-reduce.1
where the time goes:
time: 705 us; the launch traced here: 703 us
  waiting for transfers between devices  508 us (72%)
  other arithmetic  54 us (8%)
  starting transfers between devices  50.4 us (7%)
  local copies, waits for them, and re-layouts  39.1 us (6%)
  matrix products  16.5 us (2%)
  blocking collectives  14.6 us (2%)
  between operations  14.5 us (2%)
    psum x1, waiting for transfers between devices, shards(): grad_short = lax.psum(jnp.stack(partial_short), ('ctx', 'dp'))  425 us
    all_to_all x1, waiting for transfers between devices, shards(): lax.all_to_all(back_rows, 'ctx', split_axis=0, concat_axis=1, tiled=True)  27.9 us
    all_to_all x1, waiting for transfers between devices, shards(): lax.all_to_all(d_conv, 'ctx', split_axis=1, concat_axis=0, tiled=True)  27.1 us
    reduce_sum x8, other arithmetic, one_mode(): grad_row = jnp.sum(forward * cot_f, axis=(1, 2))  25.3 us
    all_to_all x1, waiting for transfers between devices, shards(): lax.all_to_all(gated, 'ctx', split_axis=1, concat_axis=0, tiled=True)  24.2 us
    all_to_all x1, starting transfers between devices, shards(): lax.all_to_all(gated, 'ctx', split_axis=1, concat_axis=0, tiled=True)  18.3 us
    unnamed x46, local copies, waits for them, and re-layouts  15 us
    psum x1, blocking collectives, shards(): grad_residue = lax.psum(partial_value, 'dp')  14.6 us
  transfers between devices with their start and end apart: 7, of which 6 were waited for; matrix products, arithmetic and copies ran while one was open for 5% of the time, Pallas kernels for 0%

commit v1 on v0

--- a/solution.py
+++ b/solution.py
@@ -141,7 +141,7 @@
                 ]
             )
         )
-    grad_short = lax.psum(jnp.stack(partial_short), ("ctx", "dp"))
+    grad_short = lax.psum(lax.psum(jnp.stack(partial_short), "dp"), "ctx")
     return (mixed[None], grads[0], grads[1], grads[2], grad_residue, grad_short)
 
 

time: 705 us -> 598 us (0.85); the launches traced: 703 us -> 587 us
  waiting for transfers between devices: 508 us -> 390 us
    psum x1 -> x2, waiting for transfers between devices: 425 us -> 307 us  [shards(): grad_short = lax.psum(lax.psum(jnp.stack(partial_short), 'dp'), 'ctx')]
    unnamed x46 -> x52, local copies, waits for them, and re-layouts: 15 us -> 15.1 us
  transfers between devices with their start and end apart: 7 -> 8, of which waited for: 6 -> 7; matrix products, arithmetic and copies ran while one was open for 5% -> 6% of each run, Pallas kernels for 0% -> 0%
where the time goes in v1:
time: 598 us; the launch traced here: 587 us
  waiting for transfers between devices  390 us (65%)
  other arithmetic  55.6 us (9%)
  starting transfers between devices  50.5 us (8%)
  local copies, waits for them, and re-layouts  39.1 us (7%)
  matrix products  16.5 us (3%)
  blocking collectives  14.6 us (2%)
  between operations  14.5 us (2%)
    psum x2, waiting for transfers between devices, shards(): grad_short = lax.psum(lax.psum(jnp.stack(partial_short), 'dp'), 'ctx')  307 us
    all_to_all x1, waiting for transfers between devices, shards(): lax.all_to_all(back_rows, 'ctx', split_axis=0, concat_axis=1, tiled=True)  27.9 us
    all_to_all x1, waiting for transfers between devices, shards(): lax.all_to_all(d_conv, 'ctx', split_axis=1, concat_axis=0, tiled=True)  27.1 us
    reduce_sum x8, other arithmetic, one_mode(): grad_row = jnp.sum(forward * cot_f, axis=(1, 2))  25.3 us
    all_to_all x1, waiting for transfers between devices, shards(): lax.all_to_all(gated, 'ctx', split_axis=1, concat_axis=0, tiled=True)  24.2 us
    all_to_all x1, starting transfers between devices, shards(): lax.all_to_all(gated, 'ctx', split_axis=1, concat_axis=0, tiled=True)  18.3 us
    unnamed x52, local copies, waits for them, and re-layouts  15.1 us
    psum x1, blocking collectives, shards(): grad_residue = lax.psum(partial_value, 'dp')  14.6 us
  transfers between devices with their start and end apart: 8, of which 7 were waited for; matrix products, arithmetic and copies ran while one was open for 6% of the time, Pallas kernels for 0%

profile of v1, /device:TPU:1, one launch (start us, length us, event | category | flops | bytes accessed | tf_op | source)
XLA Modules:
  0.0 586.9 jit_solution(16462427615787028086)
XLA Ops:
  7.2 0.8 slice.139
  7.9 0.8 slice.140
  8.7 0.8 slice.141
  9.5 4.0 collective-permute-start
  13.6 1.0 fusion.78
  14.6 1.3 copy.33
  15.9 1.3 copy.31
  17.9 0.8 maximum_convert_fusion.1
  18.7 4.5 multiply_convert_fusion
  23.2 18.3 %all-to-all-start = ((bf16[128,64,32]{0,2,1:T(8,128)(2,1)}), bf16[128,64,32]{0,2,1:T(8,128)(2,1)S(1)}, u32[]{:S(2)}, u32[]{:S(2)}) async-start(bf16[128,64,32]{0,2,1:T(8,128)(2,1)} %bitcast.16), calls=%async_computation | async-start | bytes 1048576 | tf_op jit(solution)/shard_map/all_to_all | solution.py:95
  42.9 1.3 copy-done.4
  44.2 2.4 fusion.51
  46.6 24.2 %all-to-all-done = bf16[128,64,32]{0,2,1:T(8,128)(2,1)S(1)} async-done(((bf16[128,64,32]{0,2,1:T(8,128)(2,1)}), bf16[128,64,32]{0,2,1:T(8,128)(2,1)S(1)}, u32[]{:S(2)}, u32[]{:S(2)}) %all-to-all-start) | async-done | bytes 524320 | tf_op jit(solution)/shard_map/all_to_all | solution.py:95
  70.7 8.6 %all-to-all-start.1 = ((bf16[128,64,32]{0,2,1:T(8,128)(2,1)}), bf16[128,64,32]{0,2,1:T(8,128)(2,1)S(1)}, u32[]{:S(2)}, u32[]{:S(2)}) async-start(bf16[128,64,32]{0,2,1:T(8,128)(2,1)} %bitcast.20), calls=%async_computation.1 | async-start | bytes 1048576 | tf_op jit(solution)/shard_map/all_to_all | solution.py:96
  80.3 0.9 copy.54
  81.2 27.1 %all-to-all-done.1 = bf16[128,64,32]{0,2,1:T(8,128)(2,1)S(1)} async-done(((bf16[128,64,32]{0,2,1:T(8,128)(2,1)}), bf16[128,64,32]{0,2,1:T(8,128)(2,1)S(1)}, u32[]{:S(2)}, u32[]{:S(2)}) %all-to-all-start.1) | async-done | bytes 524320 | tf_op jit(solution)/shard_map/all_to_all | solution.py:96
  108.4 0.9 copy.55
  109.3 1.1 bitcast_convert_fusion
  110.5 60.8 %while.16 = (s32[]{:T(128)}, f32[32,64,128]{2,1,0:T(8,128)}, f32[32,64,128]{2,1,0:T(8,128)}, f32[8,32]{1,0:T(8,128)S(1)}, f32[8,32]{1,0:T(8,128)S(1)}, /*index=5...) while((s32[]{:T(128)}, f32[32,64,128]{2,1,0:T(8,128)}, ...), condition=%wide.region_2.3_spmd.clone.clone, body=%wide.region_0.2_spmd.clone.clone.sunk | while | flops 140759840 | bytes 12668891 | solution.py:58
  111.8 1.4 convolution_bitcast_fusion.5
  114.9 2.2 multiply_reduce_fusion.11
  118.4 1.4 convolution_bitcast_fusion.5
  121.5 3.3 multiply_reduce_fusion.11
  126.1 1.4 convolution_bitcast_fusion.5
  129.2 3.3 multiply_reduce_fusion.11
  133.8 1.4 convolution_bitcast_fusion.5
  137.0 3.3 multiply_reduce_fusion.11
  141.6 1.4 convolution_bitcast_fusion.5
  144.7 3.3 multiply_reduce_fusion.11
  149.3 1.4 convolution_bitcast_fusion.5
  152.4 3.3 multiply_reduce_fusion.11
  157.1 1.4 convolution_bitcast_fusion.5
  160.2 3.3 multiply_reduce_fusion.11
  164.8 1.4 convolution_bitcast_fusion.5
  167.9 3.3 multiply_reduce_fusion.11
  171.3 1.4 convert_element_type.94
  172.7 1.1 copy_bitcast_fusion
  173.8 9.2 %all-to-all-start.3 = ((bf16[64,128,32]{1,2,0:T(8,128)(2,1)}), bf16[64,128,32]{1,2,0:T(8,128)(2,1)}, u32[]{:S(2)}, u32[]{:S(2)}) async-start(bf16[64,128,32]{1,2,0:T(8,128)(2,1)} %copy_bitcast_fusion), calls=%async_computation.3 | async-start | bytes 1048576 | tf_op jit(solution)/shard_map/all_to_all | solution.py:113
  183.1 1.1 copy_bitcast_fusion.1
  184.3 27.9 %all-to-all-done.3 = bf16[64,128,32]{1,2,0:T(8,128)(2,1)} async-done(((bf16[64,128,32]{1,2,0:T(8,128)(2,1)}), bf16[64,128,32]{1,2,0:T(8,128)(2,1)}, u32[]{:S(2)}, u32[]{:S(2)}) %all-to-all-start.3) | async-done | bytes 524320 | tf_op jit(solution)/shard_map/all_to_all | solution.py:113
  212.1 8.9 %all-to-all-start.2 = ((bf16[64,128,32]{1,2,0:T(8,128)(2,1)}), bf16[64,128,32]{1,2,0:T(8,128)(2,1)}, u32[]{:S(2)}, u32[]{:S(2)}) async-start(bf16[64,128,32]{1,2,0:T(8,128)(2,1)} %copy_bitcast_fusion.1), calls=%async_computation.2 | async-start | bytes 1048576 | tf_op jit(solution)/shard_map/all_to_all | solution.py:112
  221.2 14.6 %psum.21 = f32[32,8]{0,1:T(8,128)} all-reduce(f32[32,8]{0,1:T(8,128)S(1)} %multiply_bitcast_fusion), channel_id=1, replica_groups=mesh['ctx'=64,'dp'=8] {'dp'}, use_global_device_ids=true, to_apply=%region_3.4 | all-reduce | flops 256 | bytes 2048 | tf_op jit(solution)/shard_map/psum | solution.py:115
  235.8 6.2 %multiply_reduce_fusion.6 = (f32[2048]{0:T(1024)S(1)}, f32[2048]{0:T(1024)S(1)}, f32[2048]{0:T(1024)S(1)}, f32[128,2048]{0,1:T(8,128)S(1)}, f32[2048]{0:T(1024)S...) fusion(f32[130,2048]{0,1:T(8,128)S(1)} %copy-done.2, f32[128,2048]{0,1:T(8,128)} %get-tuple-element.211, ...), kind=kLoop, calls=%fused_computation.106 | loop fusion | flops 3919872 | bytes 11059200 | tf_op jit(solution)/shard_map/reduce_sum | solution.py:136
  242.0 1.0 copy-done.7
  243.0 0.8 fusion.72
  243.9 1.2 copy.40
  245.1 0.9 fusion.73
  246.0 1.2 copy.41
  247.2 2.9 all-to-all-done.2
  250.1 3.0 multiply_reduce_fusion.9
  253.5 1.3 collective-permute-start.1
  255.6 1.0 copy.43
  256.6 1.4 collective-permute-done.1
  258.1 0.9 copy.42
  259.4 1.0 copy-done.10
  260.4 2.7 fusion.76
  263.1 2.8 fusion.75
  265.9 59.5 %all-reduce.3.cloned.1.call-done = f32[3,3,2048]{2,1,0:T(4,128)} async-done(((f32[3,3,2048]{2,1,0:T(4,128)}), f32[3,3,2048]{2,1,0:T(4,128)}) %all-reduce.3.cloned.1.call-update) | async-done | bytes 73744 | tf_op jit(solution)/shard_map/psum | solution.py:144
  325.4 2.8 fusion.74
  328.1 1.0 copy.46
  329.1 1.0 copy.45
  330.2 1.0 copy.44
  331.2 247.4 %all-reduce.5.cloned.1.call-done = f32[3,3,2048]{2,1,0:T(4,128)} async-done(((f32[3,3,2048]{2,1,0:T(4,128)}), f32[3,3,2048]{2,1,0:T(4,128)}) %all-reduce.5.cloned.1.call-update) | async-done | bytes 73744 | tf_op jit(solution)/shard_map/psum | solution.py:144
  578.6 1.5 copy.81
  (160 shorter events, 23.1 us)
Async XLA Ops:
  9.5 7.7 %collective-permute-start = (bf16[3,2,2048]{2,1,0:T(2,128)(2,1)S(1)}, bf16[3,2,2048]{2,1,0:T(2,128)(2,1)S(1)}, u32[]{:S(2)}, u32[]{:S(2)}) collective-permute-start(bf16[3,2,2048]{2,1,0:T(2,128)(2,1)S(1)} %pad_maximum_fusion.4), channel_id=1, source_target_pairs={{0,8},{8,16},{16,24},{24,32},{32,40},{40,48},{48,56},{56,64},{64,7... | collective-permute-start | bytes 73736 | tf_op jit(solution)/shard_map/ppermute | solution.py:13
  18.7 4.5 copy-start.1
  18.7 4.5 copy-start.3
  18.7 22.8 %copy-start.16 = (bf16[1,128,2048]{2,1,0:T(8,128)(2,1)S(1)}, bf16[1,128,2048]{2,1,0:T(8,128)(2,1)}, u32[]{:S(2)}) copy-start(bf16[1,128,2048]{2,1,0:T(8,128)(2,1)} %param.9) | copy-start | bytes 1572868
  23.2 18.6 %copy-start.17 = (bf16[1,128,2048]{2,1,0:T(8,128)(2,1)S(1)}, bf16[1,128,2048]{2,1,0:T(8,128)(2,1)}, u32[]{:S(2)}) copy-start(bf16[1,128,2048]{2,1,0:T(8,128)(2,1)} %param.12) | copy-start | bytes 1572868
  23.2 47.5 %all-to-all-start = ((bf16[128,64,32]{0,2,1:T(8,128)(2,1)}), bf16[128,64,32]{0,2,1:T(8,128)(2,1)S(1)}, u32[]{:S(2)}, u32[]{:S(2)}) async-start(bf16[128,64,32]{0,2,1:T(8,128)(2,1)} %bitcast.16), calls=%async_computation | async-start | bytes 1048576 | tf_op jit(solution)/shard_map/all_to_all | solution.py:95
  42.1 4.5 copy-start.11
  42.9 1.3 copy-start.4
  44.2 35.2 %copy-start.18 = (f32[8]{0:T(128)S(1)}, f32[8]{0:T(128)}, u32[]{:S(2)}) copy-start(f32[8]{0:T(128)} %param.15) | copy-start | bytes 100
  70.7 37.6 %all-to-all-start.1 = ((bf16[128,64,32]{0,2,1:T(8,128)(2,1)}), bf16[128,64,32]{0,2,1:T(8,128)(2,1)S(1)}, u32[]{:S(2)}, u32[]{:S(2)}) async-start(bf16[128,64,32]{0,2,1:T(8,128)(2,1)} %bitcast.20), calls=%async_computation.1 | async-start | bytes 1048576 | tf_op jit(solution)/shard_map/all_to_all | solution.py:96
  111.7 2.0 copy-start.6
  118.3 2.0 copy-start.6
  126.1 2.0 copy-start.6
  133.8 2.0 copy-start.6
  141.5 2.0 copy-start.6
  149.3 2.0 copy-start.6
  157.0 2.0 copy-start.6
  164.8 2.0 copy-start.6
  171.3 11.8 %copy-start = (f32[32,64,128]{2,1,0:T(8,128)S(1)}, f32[32,64,128]{2,1,0:T(8,128)}, u32[]{:S(2)}) copy-start(f32[32,64,128]{2,1,0:T(8,128)} %get-tuple-element.87) | copy-start | bytes 3145732
  173.8 38.3 %all-to-all-start.3 = ((bf16[64,128,32]{1,2,0:T(8,128)(2,1)}), bf16[64,128,32]{1,2,0:T(8,128)(2,1)}, u32[]{:S(2)}, u32[]{:S(2)}) async-start(bf16[64,128,32]{1,2,0:T(8,128)(2,1)} %copy_bitcast_fusion), calls=%async_computation.3 | async-start | bytes 1048576 | tf_op jit(solution)/shard_map/all_to_all | solution.py:113
  183.0 52.7 %copy-start.2 = (f32[130,2048]{0,1:T(8,128)S(1)}, f32[130,2048]{0,1:T(8,128)}, u32[]{:S(2)}) copy-start(f32[130,2048]{0,1:T(8,128)} %copy-done.1) | copy-start | bytes 3194884
  212.1 38.0 %all-to-all-start.2 = ((bf16[64,128,32]{1,2,0:T(8,128)(2,1)}), bf16[64,128,32]{1,2,0:T(8,128)(2,1)}, u32[]{:S(2)}, u32[]{:S(2)}) async-start(bf16[64,128,32]{1,2,0:T(8,128)(2,1)} %copy_bitcast_fusion.1), calls=%async_computation.2 | async-start | bytes 1048576 | tf_op jit(solution)/shard_map/all_to_all | solution.py:112
  221.0 104.3 %all-reduce.3.cloned.1.call-start = ((), (), s32[]{:S(2)}) async-start(), calls=%async_computation.4 | async-start | bytes 196608 | tf_op jit(solution)/shard_map/psum | solution.py:144
  242.0 1.0 copy-start.7
  242.0 8.1 %copy-start.9 = (f32[128,2048]{0,1:T(8,128)}, f32[128,2048]{0,1:T(8,128)S(1)}, u32[]{:S(2)}) copy-start(f32[128,2048]{0,1:T(8,128)S(1)} %get-tuple-element.228) | copy-start | bytes 3145732
  242.0 8.1 %copy-start.5 = (f32[130,2048]{0,1:T(8,128)S(1)}, f32[130,2048]{0,1:T(8,128)}, u32[]{:S(2)}) copy-start(f32[130,2048]{0,1:T(8,128)} %copy-done.4) | copy-start | bytes 3194884
  253.1 2.5 copy-start.15
  253.5 4.6 collective-permute-start.1
  255.6 323.0 %all-reduce.5.cloned.1.call-start = ((), (), s32[]{:S(2)}) async-start(), calls=%async_computation.5 | async-start | bytes 196608 | tf_op jit(solution)/shard_map/psum | solution.py:144
  259.1 1.2 copy-start.10
  259.4 3.8 copy-start.8
  265.9 62.3 %copy-start.12 = (bf16[1,128,2048]{1,2,0:T(8,128)(2,1)S(1)}, bf16[1,128,2048]{1,2,0:T(8,128)(2,1)}, u32[]{:S(2)}) copy-start(bf16[1,128,2048]{1,2,0:T(8,128)(2,1)} %fusion.76) | copy-start | bytes 1572868
  265.9 63.3 %copy-start.13 = (bf16[1,128,2048]{1,2,0:T(8,128)(2,1)S(1)}, bf16[1,128,2048]{1,2,0:T(8,128)(2,1)}, u32[]{:S(2)}) copy-start(bf16[1,128,2048]{1,2,0:T(8,128)(2,1)} %fusion.75) | copy-start | bytes 1572868
  328.1 2.0 copy-start.14
Sparse Core Ops, SparseCore 0:
  255.7 69.5 all-reduce.2
  329.1 249.3 all-reduce.4
